TPU v7x, 32 devices: a whole 2x2x4 slice. The times are simulated.
32 devices in a mesh: group: 2 (over y), seq: 4 (over z), head: 4 (over x, core).
Axes of the slice: x: 2, y: 2, z: 4, core: 2. Of those that a mesh axis runs over, the one named last changes fastest.
Arguments:
- tokens: bfloat16 [4096, 768], P(('group', 'seq')), parts along dimension 0, may hold values from -40 to 40
- w_qkv: bfloat16 [3, 768, 768], P(None, None, 'head'), may hold values from -1 to 1
- w_out: bfloat16 [768, 768], P('head'), may hold values from -0.75 to 0.75
- gain: float32 [768], P('head'), may hold values from 0.5 to 1.5
- bias: float32 [768], P('head'), may hold values from -3 to 3
- mid_offset: int32 [12], P('head'), may hold values from 0 to 7
- far_offset: int32 [12], P('head'), may hold values from 0 to 31
Outputs:
- encoded: bfloat16 [4096, 768], P(('group', 'seq'), 'head'), parts along dimension 0
There are 2 independent parts, one for each index of `group`. A program takes and returns all parts, laid end to end along the dimension named above; an argument that names none is the same for every part. Nothing has to cross between parts.
All inputs are finite; a program needn't handle non-finite values.
Results may differ from a plain program's by a relative error of at most 0.0085.
Values may be sent and summed in bfloat16 or wider, within the bound.
No kernel may reach another device: no remote copies, remote signals or barrier semaphores. Data moves between devices by JAX's collectives and lax.ppermute only.
A program may use at most 64 MiB of HBM per device.

v0:
```python
from functools import partial
import math
import jax
import jax.numpy as jnp
from jax import lax
from jax.sharding import PartitionSpec as P

HEADS = 12
SEG0 = 128
R1 = 8
R2 = 32
epsilon = 1e-05


def attend(queries, keys_in, values_in, scale):
    scores = (
        jnp.einsum("qhd,khd->hqk", queries, keys_in, preferred_element_type=jnp.float32) * scale
    )
    peaks = jnp.max(scores, axis=-1)
    shifted = jnp.exp(scores - peaks[..., None])
    masses = jnp.sum(shifted, axis=-1)
    weights = shifted.astype(jnp.bfloat16)
    summed = jnp.einsum("hqk,khd->qhd", weights, values_in, preferred_element_type=jnp.float32)
    result = summed / jnp.transpose(masses)[:, :, None]
    log_mass = jnp.transpose(peaks + jnp.log(masses))
    return (result, log_mass)


def pick(source, offset, rate):
    folded = source.reshape(source.shape[0] // rate, rate, source.shape[1], source.shape[2])
    chosen = lax.broadcasted_iota(jnp.int32, (rate, source.shape[1]), 0) == offset[None, :]
    kept = jnp.where(chosen[None, :, :, None], folded, jnp.zeros((), source.dtype))
    return jnp.sum(kept, axis=1)


def spread(result, log_mass, offset, rate):
    count = result.shape[0]
    chosen = lax.broadcasted_iota(jnp.int32, (rate, result.shape[1]), 0) == offset[None, :]
    full = jnp.where(chosen[None, :, :, None], result[:, None], 0.0)
    full = full.reshape(count * rate, result.shape[1], result.shape[2])
    mass_full = jnp.where(chosen[None], log_mass[:, None, :], -1e30).reshape(
        count * rate, result.shape[1]
    )
    return (full, mass_full)


def local(tokens, w_qkv, w_out, gain, bias, mid_offset, far_offset):
    rows_here = tokens.shape[0]
    width = tokens.shape[1]
    heads_here = mid_offset.shape[0]
    head_size = width // HEADS
    cols_here = heads_here * head_size
    scale = 1.0 / math.sqrt(head_size)
    projected = jnp.einsum("td,sde->ste", tokens, w_qkv, preferred_element_type=jnp.float32).astype(
        jnp.bfloat16
    )
    query = projected[0].reshape(rows_here, heads_here, head_size)
    keyed = projected[1].reshape(rows_here, heads_here, head_size)
    value = projected[2].reshape(rows_here, heads_here, head_size)
    blocks = rows_here // SEG0
    near_out, near_mass = jax.vmap(partial(attend, scale=scale))(
        query.reshape(blocks, SEG0, heads_here, head_size),
        keyed.reshape(blocks, SEG0, heads_here, head_size),
        value.reshape(blocks, SEG0, heads_here, head_size),
    )
    near_out = near_out.reshape(rows_here, heads_here, head_size)
    near_mass = near_mass.reshape(rows_here, heads_here)
    mid_count = rows_here // R1
    far_count = rows_here // R2
    mid_query = pick(query, mid_offset, R1)
    mid_stack = jnp.stack(
        [
            pick(keyed, mid_offset, R1).reshape(mid_count, cols_here),
            pick(value, mid_offset, R1).reshape(mid_count, cols_here),
        ]
    )
    far_query = pick(query, far_offset, R2)
    far_stack = jnp.stack(
        [
            pick(keyed, far_offset, R2).reshape(far_count, cols_here),
            pick(value, far_offset, R2).reshape(far_count, cols_here),
        ]
    )
    mid_devs = min(8, lax.axis_size("seq"))
    place = lax.axis_index("seq")
    gathered_mid, far_all = (
        lax.all_gather(mid_stack, "seq", axis=1, tiled=True),
        lax.all_gather(far_stack, "seq", axis=1, tiled=True),
    )
    first_row = place // mid_devs * (mid_devs * mid_count)
    mid_all = lax.dynamic_slice_in_dim(gathered_mid, first_row, mid_devs * mid_count, 1)
    mid_out, mid_mass = attend(
        mid_query,
        mid_all[0].reshape(-1, heads_here, head_size),
        mid_all[1].reshape(-1, heads_here, head_size),
        scale,
    )
    far_out, far_mass = attend(
        far_query,
        far_all[0].reshape(-1, heads_here, head_size),
        far_all[1].reshape(-1, heads_here, head_size),
        scale,
    )
    mid_full, mid_mfull = spread(mid_out, mid_mass, mid_offset, R1)
    far_full, far_mfull = spread(far_out, far_mass, far_offset, R2)
    top = jnp.maximum(jnp.maximum(near_mass, mid_mfull), far_mfull)
    near_weight = jnp.exp(near_mass - top)
    mid_weight = jnp.exp(mid_mfull - top)
    far_weight = jnp.exp(far_mfull - top)
    mixed = (
        near_weight[..., None] * near_out
        + mid_weight[..., None] * mid_full
        + far_weight[..., None] * far_full
    )
    mixed = mixed / (near_weight + mid_weight + far_weight)[..., None]
    attn = mixed.reshape(rows_here, cols_here).astype(jnp.bfloat16)
    head_count = lax.axis_size("head")
    head_place = lax.axis_index("head")
    piece_cols = width // head_count
    weight_cols = lax.all_to_all(w_out, "head", split_axis=1, concat_axis=0, tiled=True)
    summed = jnp.dot(
        lax.all_gather(attn, "head", axis=1, tiled=True),
        weight_cols,
        preferred_element_type=jnp.float32,
    )
    resid = (
        lax.dynamic_slice_in_dim(tokens, head_place * piece_cols, piece_cols, 1).astype(jnp.float32)
        + summed
    )
    totals, squares = lax.psum((jnp.sum(resid, axis=1), jnp.sum(resid * resid, axis=1)), "head")
    mean = totals / width
    var = squares / width - mean * mean
    normed_cols = (resid - mean[:, None]) * lax.rsqrt(var + epsilon)[:, None]
    return (normed_cols * gain + bias).astype(jnp.bfloat16)


def solution(mesh):
    in_specs = (
        P(("group", "seq"), None),
        P(None, None, "head"),
        P("head", None),
        P("head"),
        P("head"),
        P("head"),
        P("head"),
    )
    out_specs = P(("group", "seq"), "head")
    return jax.shard_map(local, mesh=mesh, in_specs=in_specs, out_specs=out_specs, check_vma=False)
```

profile of v0, /device:TPU:0, one launch (start us, length us, event | category | flops | bytes accessed | tf_op | source)
XLA Modules:
  0.0 76.6 jit_solution(17679054772339913622)
XLA Ops:
  0.0 2.0 %copy.128 = bf16[192,768]{0,1:T(8,128)(2,1)} copy(bf16[192,768]{1,0:T(8,128)(2,1)} %param.9) | data formatting | bytes 589824 | tf_op args[2]
  2.0 4.2 %all-to-all-start = ((bf16[192,4,192]{0,2,1:T(8,128)(2,1)}), bf16[192,4,192]{0,2,1:T(8,128)(2,1)}, u32[]{:S(2)}, u32[]{:S(2)}) async-start(bf16[192,4,192]{0,2,1:T(8,128)(2,1)} %bitcast.24), calls=%async_computation | async-start | bytes 786432 | tf_op jit(solution)/shard_map/all_to_all | solution.py:120
  6.2 0.7 fusion
  7.7 1.0 %reshape_reshape_squeeze.30 = bf16[64,8,3,64]{3,2,1,0:T(4,128)(2,1)} reshape(bf16[1,512,192]{2,1,0:T(8,128)(2,1)S(1)} %copy.104) | data formatting | bytes 393216 | tf_op jit(solution)/shard_map/reshape;reshape;squeeze | solution.py:30
  9.0 0.9 %reshape_reshape_squeeze.31 = bf16[64,8,3,64]{3,2,1,0:T(4,128)(2,1)} reshape(bf16[1,512,192]{2,1,0:T(8,128)(2,1)S(1)} %copy.106) | data formatting | bytes 393216 | tf_op jit(solution)/shard_map/reshape;reshape;squeeze | solution.py:30
  10.1 1.7 %reshape_reshape_squeeze.27 = bf16[4,128,3,64]{1,0,3,2:T(4,128)(2,1)} reshape(bf16[1,512,192]{1,2,0:T(8,128)(2,1)} %copy-done.4) | data formatting | bytes 393216 | tf_op jit(solution)/shard_map/reshape;reshape;squeeze | solution.py:62
  11.8 1.7 %reshape_reshape_squeeze.28 = bf16[4,128,3,64]{1,0,3,2:T(4,128)(2,1)} reshape(bf16[1,512,192]{1,2,0:T(8,128)(2,1)} %copy-done.3) | data formatting | bytes 393216 | tf_op jit(solution)/shard_map/reshape;reshape;squeeze | solution.py:63
  13.4 1.7 %reshape_reshape_squeeze.35 = bf16[4,128,3,64]{1,0,3,2:T(4,128)(2,1)} reshape(bf16[1,512,192]{1,2,0:T(8,128)(2,1)} %copy-done.2) | data formatting | bytes 393216 | tf_op jit(solution)/shard_map/reshape;reshape;squeeze | solution.py:64
  15.2 3.4 %select_reduce_fusion.5 = (bf16[64,3,64]{2,1,0:T(4,128)(2,1)}, bf16[64,3,64]{2,1,0:T(4,128)(2,1)}, bf16[64,3,64]{2,1,0:T(4,128)(2,1)}) fusion(bf16[64,8,3,64]{3,2,1,0:T(4,128)(2,1)S(1)} %reshape_reshape_squeeze.29, pred[8,3]{1,0:T(8,128)(4,1)S(1)} %iota_compare_fusion.1, bf16[64,8,3,64]{3,2,1,0:T(4,128)(2,1)S(1)} %copy-done.1, ...), kind=kLoop, calls=%fused_computation.21 | loop fusion | flops 552960 | bytes 663576 | tf_op jit(solution)/shard_map/reduce_sum | solution.py:33
  18.6 0.9 %copy.105 = bf16[64,3,64]{0,2,1:T(8,128)(2,1)S(1)} copy(bf16[64,3,64]{2,1,0:T(4,128)(2,1)} %get-tuple-element.11) | data formatting | bytes 49152 | tf_op jit(solution)/shard_map/reduce_sum | solution.py:33
  19.5 0.9 %copy.107 = bf16[64,3,64]{0,2,1:T(8,128)(2,1)S(1)} copy(bf16[64,3,64]{2,1,0:T(4,128)(2,1)} %get-tuple-element.12) | data formatting | bytes 49152 | tf_op jit(solution)/shard_map/reduce_sum | solution.py:33
  20.6 15.6 %all_gather.9 = bf16[2,256,192]{2,0,1:T(2,128)(2,1)S(1)} all-gather(bf16[2,64,192]{2,0,1:T(2,128)(2,1)S(1)} %copy.108), channel_id=1, replica_groups=mesh['group'=2,'seq'=4,'head'=4] {'seq'}, dimensions={1}, use_global_device_ids=true | all-gather | bytes 245760 | tf_op jit(solution)/shard_map/all_gather | solution.py:87
  36.2 0.4 fusion.31
  36.8 0.2 fusion.34
  37.5 1.1 %select_reduce_fusion.2 = (bf16[16,3,64]{2,1,0:T(4,128)(2,1)S(1)}, bf16[16,3,64]{2,1,0:T(4,128)(2,1)S(1)}, bf16[16,3,64]{2,1,0:T(4,128)(2,1)S(1)}) fusion(bf16[16,32,3,64]{3,2,1,0:T(4,128)(2,1)S(1)} %reshape_reshape_squeeze.32, pred[32,3]{1,0:T(8,128)(4,1)S(1)} %iota_compare_fusion, bf16[16,32,3,64]{3,2,1,0:T(4,128)(2,1)S(1)} %reshape_reshape_squeeze.33, ...), kind=kLoop, calls=%fused_computation.18 | loop fusion | flops 580608 | bytes 608352 | tf_op jit(solution)/shard_map/reduce_sum | solution.py:33
  38.9 13.3 %all_gather.10 = bf16[2,64,192]{2,1,0:T(8,128)(2,1)S(1)} all-gather(bf16[2,16,192]{2,1,0:T(8,128)(2,1)S(1)} %pad_maximum_fusion.1), channel_id=1, replica_groups=mesh['group'=2,'seq'=4,'head'=4] {'seq'}, dimensions={1}, use_global_device_ids=true | all-gather | bytes 61440 | tf_op jit(solution)/shard_map/all_gather | solution.py:88
  52.3 0.2 fusion.33
  53.3 0.2 fusion.2
  53.8 0.6 broadcast_in_dim.184
  54.6 0.2 fusion.3
  55.0 0.6 broadcast_in_dim.189
  56.1 0.3 fusion.35
  56.5 0.5 copy-done.8
  57.0 0.3 fusion.1
  57.2 0.3 copy.120
  57.5 1.1 %constant_dynamic-slice_fusion = bf16[512,192]{1,0:T(8,128)(2,1)S(1)} fusion(bf16[512,768]{1,0:T(8,128)(2,1)} %param.7, s32[]{:T(128)S(6)} %select_n.99), kind=kLoop, calls=%fused_computation.61 | loop fusion | bytes 393220 | tf_op jit(solution)/shard_map/dynamic_slice | solution.py:127
  59.0 8.8 %all_gather.11 = bf16[512,768]{0,1:T(8,128)(2,1)S(1)} all-gather(bf16[512,192]{0,1:T(8,128)(2,1)S(1)} %fusion.12), channel_id=1, replica_groups=mesh['group'=2,'seq'=4,'head'=4] {'head'}, dimensions={1}, use_global_device_ids=true | all-gather | bytes 983040 | tf_op jit(solution)/shard_map/all_gather | solution.py:122
  67.8 1.3 %copy.129 = bf16[4,192,192]{1,0,2:T(4,128)(2,1)S(1)} copy(bf16[4,192,192]{1,2,0:T(8,128)(2,1)} %bitcast.25) | data formatting | bytes 589824 | tf_op jit(solution)/shard_map/all_to_all | solution.py:120
  69.1 0.3 all_to_all.17
  69.4 0.3 fusion.28
  69.8 6.0 %all-reduce = (f32[512]{0:T(512)S(1)}, f32[512]{0:T(512)S(1)}) all-reduce(f32[512]{0:T(512)S(1)} %get-tuple-element.6, f32[512]{0:T(512)S(1)} %get-tuple-element.5), channel_id=1, replica_groups=mesh['group'=2,'seq'=4,'head'=4] {'head'}, use_global_device_ids=true, to_apply=%region_15.16 | all-reduce | flops 1024 | bytes 8192 | tf_op jit(solution)/shard_map/psum | solution.py:130
  75.8 0.8 %add_convert_fusion = bf16[512,192]{0,1:T(8,128)(2,1)} fusion(f32[512,192]{0,1:T(8,128)S(1)} %get-tuple-element.34, f32[192]{0:T(256)S(1)} %copy-done.10, f32[192]{0:T(256)S(1)} %copy-done.11, f32[512]{0:T(512)S(1)} %get-tuple-element.27, f32[512]{0:T(512)S(1)} %get-tuple-element.26), kind=kLoop, calls=%fused_computation.28 | loop fusion | flops 491520 | bytes 595456 | tf_op jit(solution)/shard_map/convert_element_type | solution.py:134
  (73 shorter events, 4.7 us)
Async XLA Ops:
  0.0 6.2 %copy-start = (bf16[3,768,192]{1,2,0:T(8,128)(2,1)S(1)}, bf16[3,768,192]{1,2,0:T(8,128)(2,1)}, u32[]{:S(2)}) copy-start(bf16[3,768,192]{1,2,0:T(8,128)(2,1)} %param.8) | copy-start | bytes 2654212
  0.0 6.2 %copy-start.9 = (bf16[512,768]{1,0:T(8,128)(2,1)S(1)}, bf16[512,768]{1,0:T(8,128)(2,1)}, u32[]{:S(2)}) copy-start(bf16[512,768]{1,0:T(8,128)(2,1)} %param.7) | copy-start | bytes 2359300
  2.0 65.7 %all-to-all-start = ((bf16[192,4,192]{0,2,1:T(8,128)(2,1)}), bf16[192,4,192]{0,2,1:T(8,128)(2,1)}, u32[]{:S(2)}, u32[]{:S(2)}) async-start(bf16[192,4,192]{0,2,1:T(8,128)(2,1)} %bitcast.24), calls=%async_computation | async-start | bytes 786432 | tf_op jit(solution)/shard_map/all_to_all | solution.py:120
  6.9 0.7 copy-start.3
  7.0 0.7 copy-start.4
  7.0 1.8 %copy-start.2 = (bf16[1,512,192]{1,2,0:T(8,128)(2,1)}, bf16[1,512,192]{1,2,0:T(8,128)(2,1)S(1)}, u32[]{:S(2)}) copy-start(bf16[1,512,192]{1,2,0:T(8,128)(2,1)S(1)} %get-tuple-element.19) | copy-start | bytes 589828
  9.9 5.2 %copy-start.13 = (s32[3]{0:T(128)S(1)}, s32[3]{0:T(128)}, u32[]{:S(2)}) copy-start(s32[3]{0:T(128)} %param.12) | copy-start | bytes 40
  10.0 5.1 %copy-start.1 = (bf16[64,8,3,64]{3,2,1,0:T(4,128)(2,1)S(1)}, bf16[64,8,3,64]{3,2,1,0:T(4,128)(2,1)}, u32[]{:S(2)}) copy-start(bf16[64,8,3,64]{3,2,1,0:T(4,128)(2,1)} %reshape_reshape_squeeze.30) | copy-start | bytes 589828
  20.5 16.3 %copy-start.7 = (bf16[64,3,64]{2,1,0:T(4,128)(2,1)S(1)}, bf16[64,3,64]{2,1,0:T(4,128)(2,1)}, u32[]{:S(2)}) copy-start(bf16[64,3,64]{2,1,0:T(4,128)(2,1)} %get-tuple-element.10) | copy-start | bytes 73732
  36.2 1.2 %copy-start.12 = (s32[3]{0:T(128)S(1)}, s32[3]{0:T(128)}, u32[]{:S(2)}) copy-start(s32[3]{0:T(128)} %param.13) | copy-start | bytes 40
  55.0 0.9 %copy-start.5 = (bf16[4,128,3,64]{1,0,3,2:T(4,128)(2,1)S(1)}, bf16[4,128,3,64]{1,0,3,2:T(4,128)(2,1)}, u32[]{:S(2)}) copy-start(bf16[4,128,3,64]{1,0,3,2:T(4,128)(2,1)} %reshape_reshape_squeeze.27) | copy-start | bytes 589828
  55.0 1.0 %copy-start.6 = (bf16[4,128,3,64]{1,0,3,2:T(4,128)(2,1)S(1)}, bf16[4,128,3,64]{1,0,3,2:T(4,128)(2,1)}, u32[]{:S(2)}) copy-start(bf16[4,128,3,64]{1,0,3,2:T(4,128)(2,1)} %reshape_reshape_squeeze.28) | copy-start | bytes 589828
  56.0 0.9 %copy-start.8 = (bf16[4,128,3,64]{1,0,3,2:T(4,128)(2,1)S(1)}, bf16[4,128,3,64]{1,0,3,2:T(4,128)(2,1)}, u32[]{:S(2)}) copy-start(bf16[4,128,3,64]{1,0,3,2:T(4,128)(2,1)} %reshape_reshape_squeeze.35) | copy-start | bytes 589828
  69.1 6.7 %copy-start.10 = (f32[192]{0:T(256)S(1)}, f32[192]{0:T(256)}, u32[]{:S(2)}) copy-start(f32[192]{0:T(256)} %param.11) | copy-start | bytes 2308
  69.1 6.7 %copy-start.11 = (f32[192]{0:T(256)S(1)}, f32[192]{0:T(256)}, u32[]{:S(2)}) copy-start(f32[192]{0:T(256)} %param.10) | copy-start | bytes 2308
where the time goes:
time: 77.2 us; the launch traced here: 76.6 us
  blocking collectives  43.7 us (57%)
  local copies, waits for them, and re-layouts  19.7 us (26%)
  other arithmetic  6.08 us (8%)
  starting transfers between devices  4.21 us (5%)
  matrix products  2.49 us (3%)
    all_gather x1, blocking collectives, local(): lax.all_gather(mid_stack, 'seq', axis=1, tiled=True)  15.6 us
    all_gather x1, blocking collectives, local(): lax.all_gather(far_stack, 'seq', axis=1, tiled=True)  13.3 us
    all_gather x1, blocking collectives, local(): lax.all_gather(attn, 'head', axis=1, tiled=True)  8.79 us
    psum x1, blocking collectives, local(): lax.psum((jnp.sum(resid, axis=1), jnp.sum(resid * resid, axis=1)), 'head')  6.01 us
    reduce_sum x2, other arithmetic, pick(): return jnp.sum(kept, axis=1)  4.51 us
    all_to_all x1, starting transfers between devices, local(): lax.all_to_all(w_out, 'head', split_axis=1, concat_axis=0, tiled=True)  4.21 us
    unnamed x30, local copies, waits for them, and re-layouts  3.03 us
    another operation x6, local copies, waits for them, and re-layouts, pick(): source.reshape(source.shape[0] // rate, rate, source.shape[1], source.sha...  2.48 us
  transfers between devices with their start and end apart: 1, of which 0 were waited for; matrix products, arithmetic and copies ran while one was open for 29% of the time, Pallas kernels for 0%

commit v1 on v0

--- a/solution.py
+++ b/solution.py
@@ -83,8 +83,41 @@
     )
     mid_devs = min(8, lax.axis_size("seq"))
     place = lax.axis_index("seq")
+
+    def treat_entries(obj, mesh_ax):
+        even = lax.axis_size(mesh_ax)
+        finding = lax.axis_index(mesh_ax)
+        opened, field_out, long_array = (even, finding, obj.shape[1])
+        row_list = []
+        pp = 0
+        while pp < opened:
+            row_list.append((pp, (pp + 1) % opened))
+            pp += 1
+        by_rank = []
+        pp = 0
+        while pp < opened:
+            by_rank.append((pp, (pp - 1) % opened))
+            pp += 1
+        a_next = jnp.zeros((*obj.shape[:1], opened * long_array, *obj.shape[2:]), obj.dtype)
+        a_next = lax.dynamic_update_slice_in_dim(a_next, obj, field_out * long_array, axis=1)
+        taken_in = y2 = obj
+        response = opened // 2
+        dev_i = 1
+        while dev_i < response + 1:
+            taken_in = lax.ppermute(taken_in, mesh_ax, row_list)
+            a_next = lax.dynamic_update_slice_in_dim(
+                a_next, taken_in, (field_out - dev_i) % opened * long_array, axis=1
+            )
+            if dev_i < opened - response:
+                y2 = lax.ppermute(y2, mesh_ax, perm=by_rank)
+                a_next = lax.dynamic_update_slice_in_dim(
+                    a_next, y2, (field_out + dev_i) % opened * long_array, axis=1
+                )
+            dev_i += 1
+        return a_next
+
     gathered_mid, far_all = (
-        lax.all_gather(mid_stack, "seq", axis=1, tiled=True),
+        treat_entries(mid_stack, "seq"),
         lax.all_gather(far_stack, "seq", axis=1, tiled=True),
     )
     first_row = place // mid_devs * (mid_devs * mid_count)

time: 77.2 us -> 68.9 us (0.89)
  blocking collectives: 43.7 us -> 28.3 us
  starting transfers between devices: 4.21 us -> 9.38 us
  matrix products: 2.49 us -> 4.38 us
    all_gather x1 -> x0, blocking collectives: 15.6 us -> none  [local(): lax.all_gather(mid_stack, 'seq', axis=1, tiled=True)]
    dynamic_update_slice x0 -> x4, local copies, waits for them, and re-layouts: none -> 5.63 us  [the longest x2 2.78 us: treat_entries(): lax.dynamic_update_slice_in_dim(a_next, taken_in, (field_out - dev_i) % o...]
    ppermute x0 -> x3, starting transfers between devices: none -> 5.28 us  [the longest x2 3.25 us: treat_entries(): taken_in = lax.ppermute(taken_in, mesh_ax, row_list)]
    unnamed x30 -> x26, local copies, waits for them, and re-layouts: 3.03 us -> 5.82 us
    another operation x1, local copies, waits for them, and re-layouts: 1.71 us -> 0.05 us  [local(): query.reshape(blocks, SEG0, heads_here, head_size)]
    another operation x1, local copies, waits for them, and re-layouts: 1.66 us -> 0.05 us  [local(): keyed.reshape(blocks, SEG0, heads_here, head_size)]
    another operation x6, local copies, waits for them, and re-layouts: 2.48 us -> 0.87 us  [pick(): source.reshape(source.shape[0] // rate, rate, source.shape[1], source.sha...]
    another operation x1, local copies, waits for them, and re-layouts: 1.65 us -> 0.05 us  [local(): value.reshape(blocks, SEG0, heads_here, head_size)]
  transfers between devices with their start and end apart: 1 -> 4, of which waited for: 0 -> 0; matrix products, arithmetic and copies ran while one was open for 29% -> 26% of each run, Pallas kernels for 0% -> 0%
where the time goes in v1:
time: 68.9 us; the launch traced here: 68.3 us
  blocking collectives  28.3 us (41%)
  local copies, waits for them, and re-layouts  20.1 us (29%)
  starting transfers between devices  9.38 us (14%)
  other arithmetic  5.56 us (8%)
  matrix products  4.38 us (6%)
    all_gather x1, blocking collectives, local(): lax.all_gather(far_stack, 'seq', axis=1, tiled=True)  13.1 us
    all_gather x1, blocking collectives, local(): lax.all_gather(attn, 'head', axis=1, tiled=True)  9.21 us
    psum x1, blocking collectives, local(): lax.psum((jnp.sum(resid, axis=1), jnp.sum(resid * resid, axis=1)), 'head')  6.01 us
    unnamed x26, local copies, waits for them, and re-layouts  5.82 us
    all_to_all x1, starting transfers between devices, local(): lax.all_to_all(w_out, 'head', split_axis=1, concat_axis=0, tiled=True)  4.1 us
    reduce_sum x2, other arithmetic, pick(): return jnp.sum(kept, axis=1)  3.37 us
    ppermute x2, starting transfers between devices, treat_entries(): taken_in = lax.ppermute(taken_in, mesh_ax, row_list)  3.25 us
    dynamic_update_slice x2, local copies, waits for them, and re-layouts, treat_entries(): lax.dynamic_update_slice_in_dim(a_next, taken_in, (field_out - dev_i) % o...  2.78 us
  transfers between devices with their start and end apart: 4, of which 0 were waited for; matrix products, arithmetic and copies ran while one was open for 26% of the time, Pallas kernels for 0%

profile of v1, /device:TPU:0, one launch (start us, length us, event | category | flops | bytes accessed | tf_op | source)
XLA Modules:
  0.0 68.3 jit_solution(11260870563422977276)
XLA Ops:
  0.0 1.2 %copy-done = bf16[3,768,192]{1,2,0:T(8,128)(2,1)S(1)} copy-done((bf16[3,768,192]{1,2,0:T(8,128)(2,1)S(1)}, bf16[3,768,192]{1,2,0:T(8,128)(2,1)}, u32[]{:S(2)}) %copy-start) | copy-done | bytes 884760
  1.2 1.8 %fusion = bf16[3,512,192]{1,2,0:T(8,128)(2,1)S(1)} fusion(bf16[3,768,192]{1,2,0:T(8,128)(2,1)S(1)} %copy-done, bf16[512,768]{1,0:T(8,128)(2,1)} %param.7), kind=kOutput, calls=%fused_computation.2 | convolution fusion | flops 453279744 | bytes 2260992 | tf_op jit(solution)/shard_map/td,sde->ste/dot_general | solution.py:54
  3.3 0.4 copy-done.3
  4.5 2.2 %select_reduce_fusion.5 = (bf16[64,3,64]{2,1,0:T(4,128)(2,1)}, bf16[64,3,64]{2,1,0:T(4,128)(2,1)}, bf16[64,3,64]{2,1,0:T(4,128)(2,1)S(1)}) fusion(bf16[64,8,3,64]{3,2,1,0:T(4,128)(2,1)S(1)} %reshape_reshape_squeeze.29, pred[8,3]{1,0:T(8,128)(4,1)S(1)} %iota_compare_fusion.1, bf16[64,8,3,64]{3,2,1,0:T(4,128)(2,1)S(1)} %reshape_reshape_squeeze.30, ...), kind=kLoop, calls=%fused_computation.21 | loop fusion | flops 552960 | bytes 663576 | tf_op jit(solution)/shard_map/reduce_sum | solution.py:33
  6.7 0.9 %copy.103 = bf16[64,3,64]{0,2,1:T(8,128)(2,1)S(1)} copy(bf16[64,3,64]{2,1,0:T(4,128)(2,1)} %get-tuple-element.11) | data formatting | bytes 49152 | tf_op jit(solution)/shard_map/reduce_sum | solution.py:33
  7.8 0.7 pad_maximum_fusion
  8.4 3.0 %collective-permute-start = (bf16[2,64,192]{1,2,0:T(8,128)(2,1)}, bf16[2,64,192]{1,2,0:T(8,128)(2,1)}, u32[]{:S(2)}, u32[]{:S(2)}) collective-permute-start(bf16[2,64,192]{1,2,0:T(8,128)(2,1)} %pad_maximum_fusion), channel_id=1, source_target_pairs={{0,4},{4,8},{8,12},{12,0},{1,5},{5,9},{9,13},{13,1},{2,6},{6,10},{... | collective-permute-start | bytes 147464 | tf_op jit(solution)/shard_map/ppermute | solution.py:107
  11.5 2.0 %collective-permute-start.1 = (bf16[2,64,192]{1,2,0:T(8,128)(2,1)}, bf16[2,64,192]{1,2,0:T(8,128)(2,1)}, u32[]{:S(2)}, u32[]{:S(2)}) collective-permute-start(bf16[2,64,192]{1,2,0:T(8,128)(2,1)} %pad_maximum_fusion), channel_id=1, source_target_pairs={{0,12},{4,0},{8,4},{12,8},{1,13},{5,1},{9,5},{13,9},{2,14},{6,2},{... | collective-permute-start | bytes 147464 | tf_op jit(solution)/shard_map/ppermute | solution.py:112
  13.5 1.9 %copy.123 = bf16[192,768]{0,1:T(8,128)(2,1)} copy(bf16[192,768]{1,0:T(8,128)(2,1)} %param.9) | data formatting | bytes 589824 | tf_op args[2]
  15.4 4.1 %all-to-all-start = ((bf16[192,4,192]{0,2,1:T(8,128)(2,1)}), bf16[192,4,192]{0,2,1:T(8,128)(2,1)}, u32[]{:S(2)}, u32[]{:S(2)}) async-start(bf16[192,4,192]{0,2,1:T(8,128)(2,1)} %bitcast.24), calls=%async_computation | async-start | bytes 786432 | tf_op jit(solution)/shard_map/all_to_all | solution.py:153
  20.0 0.4 copy-done.4
  20.7 1.1 %select_reduce_fusion.2 = (bf16[16,3,64]{2,1,0:T(4,128)(2,1)S(1)}, bf16[16,3,64]{2,1,0:T(4,128)(2,1)S(1)}, bf16[16,3,64]{2,1,0:T(4,128)(2,1)S(1)}) fusion(bf16[16,32,3,64]{3,2,1,0:T(4,128)(2,1)S(1)} %reshape_reshape_squeeze.32, pred[32,3]{1,0:T(8,128)(4,1)S(1)} %iota_compare_fusion, bf16[16,32,3,64]{3,2,1,0:T(4,128)(2,1)S(1)} %reshape_reshape_squeeze.33, ...), kind=kLoop, calls=%fused_computation.18 | loop fusion | flops 580608 | bytes 608352 | tf_op jit(solution)/shard_map/reduce_sum | solution.py:33
  22.1 13.1 %all_gather.6 = bf16[2,64,192]{2,1,0:T(8,128)(2,1)S(1)} all-gather(bf16[2,16,192]{2,1,0:T(8,128)(2,1)S(1)} %pad_maximum_fusion.1), channel_id=1, replica_groups=mesh['group'=2,'seq'=4,'head'=4] {'seq'}, dimensions={1}, use_global_device_ids=true | all-gather | bytes 61440 | tf_op jit(solution)/shard_map/all_gather | solution.py:121
  35.8 0.3 fusion.35
  36.5 1.0 %fusion.1 = f32[4,128,3,64]{1,3,2,0:T(8,128)} fusion(f32[4,3,128,128]{2,3,1,0:T(8,128)S(1)} %get-tuple-element.33, f32[4,3,128]{2,1,0:T(4,128)S(1)} %get-tuple-element.32, bf16[4,128,3,64]{1,0,3,2:T(4,128)(2,1)S(1)} %reshape_reshape_squeeze.35, f32[4,128,3]{1,2,0:T(4,128)S(1)} %bitcast.120), kind=kOutput, calls=%fused_computation.4 | convolution fusion | flops 25657344 | bytes 1388544 | tf_op jit(solution)/shard_map/vmap(hqk,khd->qhd)/dot_general | solution.py:23
  37.7 1.1 %constant_dynamic-slice_fusion = bf16[512,192]{1,0:T(8,128)(2,1)S(1)} fusion(bf16[512,768]{1,0:T(8,128)(2,1)} %param.7, s32[]{:T(128)S(6)} %select_n.125), kind=kLoop, calls=%fused_computation.61 | loop fusion | bytes 393220 | tf_op jit(solution)/shard_map/dynamic_slice | solution.py:160
  39.7 0.6 broadcast_in_dim.193
  40.4 0.8 %copy-done.6 = f32[4,128,3,64]{1,3,2,0:T(8,128)S(1)} copy-done((f32[4,128,3,64]{1,3,2,0:T(8,128)S(1)}, f32[4,128,3,64]{1,3,2,0:T(8,128)}, u32[]{:S(2)}) %copy-start.6) | copy-done | bytes 393240
  41.3 0.3 copy.116
  41.5 0.8 %copy.128 = bf16[512,192]{0,1:T(8,128)(2,1)} copy(bf16[512,192]{1,0:T(8,128)(2,1)S(1)} %constant_dynamic-slice_fusion) | data formatting | bytes 393216
  42.3 1.2 %dynamic_update_slice.12 = bf16[2,256,192]{1,2,0:T(8,128)(2,1)S(1)} dynamic-update-slice(bf16[2,256,192]{1,2,0:T(8,128)(2,1)S(1)} %broadcast_in_dim.175, bf16[2,64,192]{1,2,0:T(8,128)(2,1)} %pad_maximum_fusion, s32[]{:T(128)} %constant.58.clone.1, s32[]{:T(128)S(6)} %select_n.129, s32[]{:T(128)} %constant.58.clone.1) | dynamic-update-slice | bytes 98308 | tf_op jit(solution)/shard_map/dynamic_update_slice | solution.py:102
  43.5 1.6 %dynamic_update_slice.13 = bf16[2,256,192]{1,2,0:T(8,128)(2,1)S(1)} dynamic-update-slice(bf16[2,256,192]{1,2,0:T(8,128)(2,1)S(1)} %dynamic_update_slice.12, bf16[2,64,192]{1,2,0:T(8,128)(2,1)} %collective-permute-done, s32[]{:T(128)} %constant.58.clone.1, s32[]{:T(128)S(6)} %select_n.131, s32[]{:T(128)} %constant.58.clone.1) | dynamic-update-slice | bytes 98308 | tf_op jit(solution)/shard_map/dynamic_update_slice | solution.py:108
  45.2 1.7 %dynamic_update_slice.14 = bf16[2,256,192]{1,2,0:T(8,128)(2,1)S(1)} dynamic-update-slice(bf16[2,256,192]{1,2,0:T(8,128)(2,1)S(1)} %dynamic_update_slice.13, bf16[2,64,192]{1,2,0:T(8,128)(2,1)} %collective-permute-done.1, s32[]{:T(128)} %constant.58.clone.1, s32[]{:T(128)S(6)} %select_n.133, s32[]{:T(128)} %constant.58.clone.1) | dynamic-update-slice | bytes 98308 | tf_op jit(solution)/shard_map/dynamic_update_slice | solution.py:113
  46.9 1.2 %dynamic_update_slice.15 = bf16[2,256,192]{1,2,0:T(8,128)(2,1)S(1)} dynamic-update-slice(bf16[2,256,192]{1,2,0:T(8,128)(2,1)S(1)} %dynamic_update_slice.14, bf16[2,64,192]{1,2,0:T(8,128)(2,1)} %collective-permute-done.2, s32[]{:T(128)} %constant.58.clone.1, s32[]{:T(128)S(6)} %select_n.135, s32[]{:T(128)} %constant.58.clone.1) | dynamic-update-slice | bytes 98308 | tf_op jit(solution)/shard_map/dynamic_update_slice | solution.py:108
  48.1 0.2 fusion.34
  49.2 0.6 broadcast_in_dim.188
  50.2 9.2 %all_gather.7 = bf16[512,768]{0,1:T(8,128)(2,1)S(1)} all-gather(bf16[512,192]{0,1:T(8,128)(2,1)S(1)} %fusion.12), channel_id=1, replica_groups=mesh['group'=2,'seq'=4,'head'=4] {'head'}, dimensions={1}, use_global_device_ids=true | all-gather | bytes 983040 | tf_op jit(solution)/shard_map/all_gather | solution.py:155
  59.4 1.3 %copy.124 = bf16[4,192,192]{1,0,2:T(4,128)(2,1)S(1)} copy(bf16[4,192,192]{1,2,0:T(8,128)(2,1)} %bitcast.25) | data formatting | bytes 589824 | tf_op jit(solution)/shard_map/all_to_all | solution.py:153
  60.7 0.3 all_to_all.17
  61.1 0.3 fusion.28
  61.4 6.0 %all-reduce = (f32[512]{0:T(512)S(1)}, f32[512]{0:T(512)S(1)}) all-reduce(f32[512]{0:T(512)S(1)} %get-tuple-element.6, f32[512]{0:T(512)S(1)} %get-tuple-element.5), channel_id=1, replica_groups=mesh['group'=2,'seq'=4,'head'=4] {'head'}, use_global_device_ids=true, to_apply=%region_15.16 | all-reduce | flops 1024 | bytes 8192 | tf_op jit(solution)/shard_map/psum | solution.py:163
  67.5 0.8 %add_convert_fusion = bf16[512,192]{0,1:T(8,128)(2,1)} fusion(f32[512,192]{0,1:T(8,128)S(1)} %get-tuple-element.34, f32[192]{0:T(256)S(1)} %copy-done.8, f32[192]{0:T(256)S(1)} %copy-done.9, f32[512]{0:T(512)S(1)} %get-tuple-element.27, f32[512]{0:T(512)S(1)} %get-tuple-element.26), kind=kLoop, calls=%fused_computation.28 | loop fusion | flops 491520 | bytes 595456 | tf_op jit(solution)/shard_map/convert_element_type | solution.py:167
  (76 shorter events, 5.5 us)
Async XLA Ops:
  0.0 1.2 %copy-start = (bf16[3,768,192]{1,2,0:T(8,128)(2,1)S(1)}, bf16[3,768,192]{1,2,0:T(8,128)(2,1)}, u32[]{:S(2)}) copy-start(bf16[3,768,192]{1,2,0:T(8,128)(2,1)} %param.8) | copy-start | bytes 2654212
  3.0 0.7 copy-start.3
  3.0 1.0 %copy-start.1 = (bf16[1,512,192]{1,2,0:T(8,128)(2,1)}, bf16[1,512,192]{1,2,0:T(8,128)(2,1)S(1)}, u32[]{:S(2)}) copy-start(bf16[1,512,192]{1,2,0:T(8,128)(2,1)S(1)} %get-tuple-element.20) | copy-start | bytes 589828
  3.8 0.7 copy-start.11
  8.4 29.1 %collective-permute-start = (bf16[2,64,192]{1,2,0:T(8,128)(2,1)}, bf16[2,64,192]{1,2,0:T(8,128)(2,1)}, u32[]{:S(2)}, u32[]{:S(2)}) collective-permute-start(bf16[2,64,192]{1,2,0:T(8,128)(2,1)} %pad_maximum_fusion), channel_id=1, source_target_pairs={{0,4},{4,8},{8,12},{12,0},{1,5},{5,9},{9,13},{13,1},{2,6},{6,10},{... | collective-permute-start | bytes 147464 | tf_op jit(solution)/shard_map/ppermute | solution.py:107
  11.5 33.7 %collective-permute-start.1 = (bf16[2,64,192]{1,2,0:T(8,128)(2,1)}, bf16[2,64,192]{1,2,0:T(8,128)(2,1)}, u32[]{:S(2)}, u32[]{:S(2)}) collective-permute-start(bf16[2,64,192]{1,2,0:T(8,128)(2,1)} %pad_maximum_fusion), channel_id=1, source_target_pairs={{0,12},{4,0},{8,4},{12,8},{1,13},{5,1},{9,5},{13,9},{2,14},{6,2},{... | collective-permute-start | bytes 147464 | tf_op jit(solution)/shard_map/ppermute | solution.py:112
  15.4 44.0 %all-to-all-start = ((bf16[192,4,192]{0,2,1:T(8,128)(2,1)}), bf16[192,4,192]{0,2,1:T(8,128)(2,1)}, u32[]{:S(2)}, u32[]{:S(2)}) async-start(bf16[192,4,192]{0,2,1:T(8,128)(2,1)} %bitcast.24), calls=%async_computation | async-start | bytes 786432 | tf_op jit(solution)/shard_map/all_to_all | solution.py:153
  19.5 0.9 %copy-start.4 = (bf16[1,512,192]{1,2,0:T(8,128)(2,1)S(1)}, bf16[1,512,192]{1,2,0:T(8,128)(2,1)}, u32[]{:S(2)}) copy-start(bf16[1,512,192]{1,2,0:T(8,128)(2,1)} %copy-done.3) | copy-start | bytes 589828
  19.7 1.0 %copy-start.2 = (bf16[1,512,192]{1,2,0:T(8,128)(2,1)S(1)}, bf16[1,512,192]{1,2,0:T(8,128)(2,1)}, u32[]{:S(2)}) copy-start(bf16[1,512,192]{1,2,0:T(8,128)(2,1)} %copy-done.1) | copy-start | bytes 589828
  19.8 0.9 %copy-start.10 = (s32[3]{0:T(128)S(1)}, s32[3]{0:T(128)}, u32[]{:S(2)}) copy-start(s32[3]{0:T(128)} %param.13) | copy-start | bytes 40
  37.5 9.4 %collective-permute-start.2 = (bf16[2,64,192]{1,2,0:T(8,128)(2,1)}, bf16[2,64,192]{1,2,0:T(8,128)(2,1)}, u32[]{:S(2)}, u32[]{:S(2)}) collective-permute-start(bf16[2,64,192]{1,2,0:T(8,128)(2,1)} %collective-permute-done), channel_id=1, source_target_pairs={{0,4},{4,8},{8,12},{12,0},{1,5},{5,9},{9,13},{13,1},{2,6},{6,10},{... | collective-permute-start | bytes 147464 | tf_op jit(solution)/shard_map/ppermute | solution.py:107
  40.3 1.0 %copy-start.6 = (f32[4,128,3,64]{1,3,2,0:T(8,128)S(1)}, f32[4,128,3,64]{1,3,2,0:T(8,128)}, u32[]{:S(2)}) copy-start(f32[4,128,3,64]{1,3,2,0:T(8,128)} %fusion.1) | copy-start | bytes 1179652
  41.5 6.6 %copy-start.7 = (bf16[64,3,64]{2,1,0:T(4,128)(2,1)S(1)}, bf16[64,3,64]{2,1,0:T(4,128)(2,1)}, u32[]{:S(2)}) copy-start(bf16[64,3,64]{2,1,0:T(4,128)(2,1)} %get-tuple-element.10) | copy-start | bytes 73732
  50.2 10.9 %copy-start.5 = (bf16[512,192]{0,1:T(8,128)(2,1)S(1)}, bf16[512,192]{0,1:T(8,128)(2,1)}, u32[]{:S(2)}) copy-start(bf16[512,192]{0,1:T(8,128)(2,1)} %copy.128) | copy-start | bytes 589828
  60.7 6.8 %copy-start.8 = (f32[192]{0:T(256)S(1)}, f32[192]{0:T(256)}, u32[]{:S(2)}) copy-start(f32[192]{0:T(256)} %param.11) | copy-start | bytes 2308
  60.7 6.7 %copy-start.9 = (f32[192]{0:T(256)S(1)}, f32[192]{0:T(256)}, u32[]{:S(2)}) copy-start(f32[192]{0:T(256)} %param.10) | copy-start | bytes 2308
